TPU v7x, 32 devices: a whole 2x2x4 slice. The times are simulated.
32 devices in a mesh: groups: 2 (over y), bx: 4 (over z), by: 2 (over x), bz: 2 (over core).
Axes of the slice: x: 2, y: 2, z: 4, core: 2. Of those that a mesh axis runs over, the one named last changes fastest.
Arguments:
- slab: float32 [4, 512, 1024], P(('groups', 'bz'), 'bx', 'by'), parts along dimension 0, may hold values from -6 to 6
- plane_test: float32 [2, 256], P('bz'), may hold values from -4 to 4
- row_test: float32 [512, 256], P('bx'), may hold values from -0.25 to 0.25
- col_test: float32 [1024, 256], P('by'), may hold values from -0.1875 to 0.1875
- core_planes: float32 [512, 2], P('bz'), may hold values from -4 to 4
- core_rows: float32 [512, 512], P(None, 'bx'), may hold values from -0.25 to 0.25
- core_cols: float32 [512, 1024], P(None, 'by'), may hold values from -0.1875 to 0.1875
Outputs:
- plane_sketch: float32 [4, 256], P(('groups', 'bz')), parts along dimension 0
- row_sketch: float32 [1024, 256], P(('groups', 'bx'), ('by', 'bz')), parts along dimension 0
- col_sketch: float32 [2048, 256], P(('groups', 'by'), ('bx', 'bz')), parts along dimension 0
- core_sketch: float32 [1024, 512, 512], P(('groups', 'bz'), 'bx', 'by'), parts along dimension 0
There are 2 independent parts, one for each index of `groups`. A program takes and returns all parts, laid end to end along the dimension named above; an argument that names none is the same for every part. Nothing has to cross between parts.
All inputs are finite; a program needn't handle non-finite values.
Results may differ from a plain program's by a relative error of at most 0.00011.
Values sent between devices are 32-bit elements; how exact they have to be, the bound alone decides.
A program may use at most 128 MiB of HBM per device.

v0:
```python
import jax
import jax.numpy as jnp
from jax import lax
from jax.sharding import PartitionSpec as P


def on_device(slab, plane_test, row_test, col_test, core_planes, core_rows, core_cols):
    highest = lax.Precision.HIGHEST
    by_col = jnp.einsum("pij,jr->pir", slab, col_test, precision=highest)
    plane_part = jnp.einsum("pir,ir->pr", by_col, row_test, precision=highest)
    row_part = jnp.einsum("pir,pr->ir", by_col, plane_test, precision=highest)
    by_row = jnp.einsum("pij,ir->pjr", slab, row_test, precision=highest)
    col_part = jnp.einsum("pjr,pr->jr", by_row, plane_test, precision=highest)
    plane_sketch = lax.psum(plane_part, ("bx", "by"))
    row_sketch = lax.psum_scatter(row_part, ("by", "bz"), scatter_dimension=1, tiled=True)
    col_sketch = lax.psum_scatter(col_part, ("bx", "bz"), scatter_dimension=1, tiled=True)
    shrunk = jnp.einsum("pij,bj->pib", slab, core_cols, precision=highest)
    reduced = lax.psum_scatter(shrunk, "by", scatter_dimension=2, tiled=True)
    partial_value = jnp.einsum("pib,ai->pab", reduced, core_rows, precision=highest)
    partial_value = lax.psum_scatter(partial_value, "bx", scatter_dimension=1, tiled=True)
    core_sketch = jnp.einsum(
        "cp,pab->cab",
        core_planes,
        lax.all_gather(partial_value, "bz", axis=0, tiled=True),
        precision=highest,
    )
    return (plane_sketch, row_sketch, col_sketch, core_sketch)


def solution(mesh):
    in_specs = (
        P(("groups", "bz"), "bx", "by"),
        P("bz", None),
        P("bx", None),
        P("by", None),
        P("bz", None),
        P(None, "bx"),
        P(None, "by"),
    )
    out_specs = (
        P(("groups", "bz"), None),
        P(("groups", "bx"), ("by", "bz")),
        P(("groups", "by"), ("bx", "bz")),
        P(("groups", "bz"), "bx", "by"),
    )
    return jax.shard_map(
        on_device, mesh=mesh, in_specs=in_specs, out_specs=out_specs, check_vma=False
    )
```

profile of v0, /device:TPU:0, one launch (start us, length us, event | category | flops | bytes accessed | tf_op | source)
XLA Modules:
  0.0 129.5 jit_solution(7191022147818254434)
XLA Ops:
  7.2 0.0 copy-start
  7.2 0.0 reduce-scatter.9.cloned.1.call-start
  7.2 1.2 copy-done
  8.4 2.8 %convolution_bitcast_fusion.2 = f32[1,128,512]{2,1,0:T(8,128)} fusion(f32[512,512]{1,0:T(8,128)S(1)} %copy-done, f32[1,128,512]{2,1,0:T(8,128)} %param.7), kind=kOutput, calls=%fused_computation.4 | convolution fusion | flops 402653184 | bytes 1572864 | tf_op jit(solution)/shard_map/pij,bj->pib/dot_general | solution.py:17
  11.2 0.0 reduce-scatter.9.cloned.1.call-update
  11.2 0.0 reduce-scatter.11.cloned.1.call-start
  11.3 14.5 %reduce-scatter.9.cloned.1.call-done = f32[1,128,256]{2,1,0:T(8,128)} async-done(((f32[1,128,512]{2,1,0:T(8,128)}), f32[1,128,256]{2,1,0:T(8,128)}) %reduce-scatter.9.cloned.1.call-update) | async-done | bytes 131088 | tf_op jit(solution)/shard_map/reduce_scatter | solution.py:18
  25.8 2.4 %convolution_bitcast_fusion.1 = f32[1,512,256]{1,2,0:T(8,128)} fusion(f32[512,128]{1,0:T(8,128)} %param.12, f32[1,128,256]{2,1,0:T(8,128)} %reduce-scatter.9.cloned.1.call-done), kind=kOutput, calls=%fused_computation.1 | convolution fusion | flops 201326592 | bytes 917504 | tf_op jit(solution)/shard_map/pib,ai->pab/dot_general | solution.py:19
  28.2 0.0 reduce-scatter.11.cloned.1.call-update
  28.2 0.0 reduce-scatter.13.cloned.1.call-start
  28.3 1.6 %multiply_reduce_fusion = (f32[256]{0:T(256)S(1)}, f32[128,256]{1,0:T(8,128)S(1)}) fusion(f32[128,256]{1,0:T(8,128)} %param.9, f32[512,256]{1,0:T(8,128)} %param.10, f32[1,128,512]{2,1,0:T(8,128)} %param.7), kind=kOutput, calls=%fused_computation.11 | convolution fusion | flops 201391872 | bytes 1049600 | tf_op jit(solution)/shard_map/pij,jr->pir/dot_general | solution.py:9
  29.9 0.7 broadcast_multiply_fusion
  30.5 0.7 copy.24
  31.3 0.0 reduce-scatter.13.cloned.1.call-update
  31.3 0.0 reduce-scatter.7.cloned.1.call-start
  31.4 2.4 %fusion = f32[512,256]{0,1:T(8,128)} fusion(f32[128,256]{1,0:T(8,128)} %param.9, f32[1,128,512]{2,1,0:T(8,128)} %param.7, f32[256]{0:T(256)} %bitcast.40), kind=kOutput, calls=%fused_computation.3 | convolution fusion | flops 201457664 | bytes 918528 | tf_op jit(solution)/shard_map/pij,ir->pjr/dot_general | solution.py:12
  33.8 0.0 reduce-scatter.7.cloned.1.call-update
  33.8 21.1 %psum.7 = f32[1,256]{1,0:T(1,128)} all-reduce(f32[1,256]{1,0:T(1,128)S(1)} %bitcast.38), channel_id=1, replica_groups=mesh['groups'=2,'bx'=4,'by'=2,'bz'=2] {'bx','by'}, use_global_device_ids=true, to_apply=%region_0.0 | all-reduce | flops 256 | bytes 2048 | tf_op jit(solution)/shard_map/psum | solution.py:14
  54.9 0.0 reduce-scatter.11.cloned.1.call-done
  54.9 1.0 copy.14
  55.9 2.0 %all_gather.3 = f32[2,128,256]{2,1,0:T(8,128)S(1)} all-gather(f32[1,128,256]{2,1,0:T(8,128)S(1)} %copy.14), channel_id=1, replica_groups=mesh['groups'=2,'bx'=4,'by'=2,'bz'=2] {'bz'}, dimensions={0}, use_global_device_ids=true | all-gather | bytes 393216 | tf_op jit(solution)/shard_map/all_gather | solution.py:24
  57.9 0.0 copy-start.1
  57.9 30.9 %convolution_bitcast_fusion = f32[256,128,256]{0,2,1:T(8,128)} fusion(f32[2,128,256]{2,1,0:T(8,128)S(1)} %all_gather.3, f32[256,2]{0,1:T(2,128)} %param.11), kind=kOutput, calls=%fused_computation | convolution fusion | flops 201326592 | bytes 33818624 | tf_op jit(solution)/shard_map/cp,pab->cab/dot_general | solution.py:21
  88.8 34.1 %copy.17 = f32[256,128,256]{2,1,0:T(8,128)} copy(f32[256,128,256]{0,2,1:T(8,128)} %convolution_bitcast_fusion) | data formatting | bytes 67108864
  122.9 0.0 reduce-scatter.13.cloned.1.call-done
  122.9 0.0 reduce-scatter.7.cloned.1.call-done
  122.9 0.0 copy-done.1
Async XLA Ops:
  7.2 1.2 copy-start
  7.2 18.6 %reduce-scatter.9.cloned.1.call-start = ((), (), s32[]{:S(2)}) async-start(), calls=%async_computation.5 | async-start | bytes 393216 | tf_op jit(solution)/shard_map/reduce_scatter | solution.py:18
  11.2 43.6 %reduce-scatter.11.cloned.1.call-start = ((), (), s32[]{:S(2)}) async-start(), calls=%async_computation.6 | async-start | bytes 655360 | tf_op jit(solution)/shard_map/reduce_scatter | solution.py:20
  28.2 94.7 %reduce-scatter.13.cloned.1.call-start = ((), (), s32[]{:S(2)}) async-start(), calls=%async_computation.7 | async-start | bytes 163840
  31.3 91.6 %reduce-scatter.7.cloned.1.call-start = ((), (), s32[]{:S(2)}) async-start(), calls=%async_computation.4 | async-start | bytes 589824 | tf_op jit(solution)/shard_map/reduce_scatter | solution.py:16
  57.9 65.0 %copy-start.1 = (f32[512,512]{1,0:T(8,128)S(1)}, f32[512,512]{1,0:T(8,128)}, u32[]{:S(2)}) copy-start(f32[512,512]{1,0:T(8,128)} %param.13) | copy-start | bytes 3145732
Sparse Core Ops, SparseCore 0:
  11.4 14.3 reduce-scatter.8
  28.7 21.6 reduce-scatter.10
  53.5 17.8 reduce-scatter.12
  74.2 30.9 reduce-scatter.6
where the time goes:
time: 130 us; the launch traced here: 129 us
  matrix products  40.2 us (31%)
  local copies, waits for them, and re-layouts  37 us (28%)
  blocking collectives  23.1 us (18%)
  waiting for transfers between devices  14.5 us (11%)
  between operations  13.8 us (11%)
    unnamed x6, local copies, waits for them, and re-layouts  36 us
    dot_general x1, matrix products, on_device(): jnp.einsum('cp,pab->cab', core_planes, lax.all_gather(partial_value, 'bz'...  30.9 us
    psum x1, blocking collectives, on_device(): plane_sketch = lax.psum(plane_part, ('bx', 'by'))  21.1 us
    reduce_scatter x1, waiting for transfers between devices, on_device(): reduced = lax.psum_scatter(shrunk, 'by', scatter_dimension=2, tiled=True)  14.5 us
    dot_general x1, matrix products, on_device(): shrunk = jnp.einsum('pij,bj->pib', slab, core_cols, precision=highest)  2.83 us
  transfers between devices with their start and end apart: 4, of which 1 were waited for; matrix products, arithmetic and copies ran while one was open for 55% of the time, Pallas kernels for 0%

commit v1 on v0

v1 whole, which is shorter than its diff:
```python
import functools

import jax
import jax.numpy as jnp
from jax import lax
from jax.experimental import pallas as pl
from jax.experimental.pallas import tpu as pltpu
from jax.sharding import PartitionSpec as P

F32 = jnp.float32
MESH = pl.DeviceIdType.MESH


def split(x):
    high = x.astype(jnp.bfloat16)
    return high, (x - high.astype(F32)).astype(jnp.bfloat16)


def dot3(a, b, dims):
    f = functools.partial(
        lax.dot_general, dimension_numbers=(dims, ((), ())), preferred_element_type=F32
    )
    return f(a[0], b[0]) + (f(a[0], b[1]) + f(a[1], b[0]))


NN = ((1,), (0,))
NT = ((1,), (1,))


def exchange_kernel(
    nx, ny, nz,
    slab_ref, plane_test_ref, row_test_ref, col_test_ref, core_rows_ref, core_cols_ref,
    gathered_ref, row_ref, col_ref, plane_ref,
    shrunk, shrunk_in, part, part_in, full, full_in,
    row_a, row_a_in, row_b, row_b_in,
    col_a, col_a_in, col_b, col_b_in,
    plane_a, plane_a_in, plane_b, plane_b_in,
    send_sem, recv_sem,
):
    size = {"bx": nx, "by": ny, "bz": nz}
    me = {name: lax.axis_index(name) for name in size}
    count = [0]

    def peer(name, d):
        return lax.rem(me[name] + d, size[name])

    barrier = pltpu.get_barrier_semaphore()
    for name in size:
        for d in range(1, size[name]):
            pl.semaphore_signal(barrier, inc=1, device_id={name: peer(name, d)}, device_id_type=MESH)

    def send(name, d, src, dst):
        n = count[0]
        count[0] += 1
        copy = pltpu.make_async_remote_copy(
            src_ref=src, dst_ref=dst, send_sem=send_sem.at[n], recv_sem=recv_sem.at[n],
            device_id={name: peer(name, d)}, device_id_type=MESH,
        )
        copy.start()
        return copy

    copies = []

    def send_all(name, source, landing):
        group = [send(name, d, source(d), landing.at[d - 1]) for d in range(1, size[name])]
        copies.extend(group)
        return group

    def arrived(group):
        for copy in group:
            copy.wait_recv()

    slab = split(slab_ref[0])
    wide = shrunk.shape[2]
    for y in range(ny):
        shrunk[y] = dot3(slab, split(core_cols_ref[y * wide:(y + 1) * wide, :]), NT)
    pl.semaphore_wait(barrier, nx + ny + nz - 3)
    shrunk_sent = send_all("by", lambda d: shrunk.at[peer("by", d)], shrunk_in)

    row_test = row_test_ref[...]
    plane_test = plane_test_ref[...]
    scaled = split((row_test * plane_test).T)
    terms = dot3(scaled, slab, NN)
    block = col_a.shape[2]
    for x in range(nx):
        for z in range(nz):
            first = (x * nz + z) * block
            col_a[z, x] = terms[first:first + block, :]
    col_a_sent = send_all("bz", lambda d: col_a.at[peer("bz", d)], col_a_in)

    by_col = dot3(slab, split(col_test_ref[...]), NN)
    plane_a[...] = jnp.sum(by_col * row_test, axis=0, keepdims=True)
    plane_a_sent = send_all("by", lambda d: plane_a, plane_a_in)
    terms = (by_col * plane_test).T
    block = row_a.shape[2]
    for y in range(ny):
        for z in range(nz):
            first = (y * nz + z) * block
            row_a[z, y] = terms[first:first + block, :]
    row_a_sent = send_all("bz", lambda d: row_a.at[peer("bz", d)], row_a_in)

    arrived(col_a_sent)
    total = col_a[me["bz"]]
    for d in range(1, nz):
        total = total + col_a_in[d - 1]
    col_b[...] = total
    col_b_sent = send_all("bx", lambda d: col_b.at[peer("bx", d)], col_b_in)

    arrived(shrunk_sent)
    total = shrunk[me["by"]]
    for d in range(1, ny):
        total = total + shrunk_in[d - 1]
    reduced = split(total)
    tall = part.shape[1]
    part_sent = []
    for d in range(1, nx + 1):
        to = peer("bx", d)
        rows = core_rows_ref[pl.ds(pl.multiple_of(to * tall, tall), tall), :]
        part[d - 1] = dot3(split(rows), reduced, NN)
        if d < nx:
            part_sent.append(send("bx", d, part.at[d - 1], part_in.at[d - 1]))
    copies.extend(part_sent)

    arrived(row_a_sent)
    total = row_a[me["bz"]]
    for d in range(1, nz):
        total = total + row_a_in[d - 1]
    row_b[...] = total
    row_b_sent = send_all("by", lambda d: row_b.at[peer("by", d)], row_b_in)

    arrived(plane_a_sent)
    total = plane_a[...]
    for d in range(1, ny):
        total = total + plane_a_in[d - 1]
    plane_b[...] = total
    plane_b_sent = send_all("bx", lambda d: plane_b, plane_b_in)

    arrived(row_b_sent)
    total = row_b[me["by"]]
    for d in range(1, ny):
        total = total + row_b_in[d - 1]
    row_ref[...] = total

    arrived(col_b_sent)
    total = col_b[me["bx"]]
    for d in range(1, nx):
        total = total + col_b_in[d - 1]
    col_ref[...] = total

    total = part[nx - 1]
    for d in range(1, nx):
        part_sent[d - 1].wait_recv()
        total = total + part_in[d - 1]
    full[...] = total
    full_sent = send_all("bz", lambda d: full, full_in)
    gathered_ref[me["bz"]] = total

    arrived(plane_b_sent)
    total = plane_b[...]
    for d in range(1, nx):
        total = total + plane_b_in[d - 1]
    plane_ref[...] = total

    arrived(full_sent)
    for d in range(1, nz):
        gathered_ref[lax.rem(me["bz"] + (nz - d), nz)] = full_in[d - 1]
    for copy in copies:
        copy.wait_send()


def core_kernel(planes_ref, gathered_ref, out_ref):
    step = pl.program_id(0)
    rows = out_ref.shape[0]
    for c in range(rows):
        row = step * rows + c
        value = planes_ref[row, 0] * gathered_ref[0]
        for p in range(1, gathered_ref.shape[0]):
            value = value + planes_ref[row, p] * gathered_ref[p]
        out_ref[c] = value


def on_device(nx, ny, nz, slab, plane_test, row_test, col_test, core_planes, core_rows, core_cols):
    rank = row_test.shape[1]
    ni, nj = slab.shape[1:]
    ab, bb = core_rows.shape[0] // nx, core_cols.shape[0] // ny
    rb, cb = rank // (ny * nz), rank // (nx * nz)
    shape = lambda *dims: jax.ShapeDtypeStruct(dims, F32)
    vmem = lambda *dims: pltpu.VMEM(dims, F32)
    transfers = 3 * (nz - 1) + 3 * (ny - 1) + 3 * (nx - 1)
    gathered, row_t, col_t, plane_sketch = pl.pallas_call(
        functools.partial(exchange_kernel, nx, ny, nz),
        out_shape=(shape(nz, ab, bb), shape(rb, ni), shape(cb, nj), shape(1, rank)),
        in_specs=[pl.BlockSpec(memory_space=pltpu.VMEM)] * 6,
        out_specs=[pl.BlockSpec(memory_space=pltpu.VMEM)] * 4,
        scratch_shapes=[
            vmem(ny, ni, bb), vmem(ny - 1, ni, bb),
            vmem(nx, ab, bb), vmem(nx - 1, ab, bb),
            vmem(ab, bb), vmem(nz - 1, ab, bb),
            vmem(nz, ny, rb, ni), vmem(nz - 1, ny, rb, ni),
            vmem(ny, rb, ni), vmem(ny - 1, rb, ni),
            vmem(nz, nx, cb, nj), vmem(nz - 1, nx, cb, nj),
            vmem(nx, cb, nj), vmem(nx - 1, cb, nj),
            vmem(1, rank), vmem(ny - 1, 1, rank),
            vmem(1, rank), vmem(nx - 1, 1, rank),
            pltpu.SemaphoreType.DMA((transfers,)),
            pltpu.SemaphoreType.DMA((transfers,)),
        ],
        compiler_params=pltpu.CompilerParams(
            collective_id=0, has_side_effects=True, vmem_limit_bytes=32 << 20
        ),
        name="exchange",
    )(slab, plane_test, row_test, col_test, core_rows, core_cols)
    depth = core_planes.shape[0]
    rows = min(depth, max(1, (1 << 19) // (ab * bb)))
    core_sketch = pl.pallas_call(
        core_kernel,
        grid=(depth // rows,),
        out_shape=shape(depth, ab, bb),
        in_specs=[
            pl.BlockSpec(memory_space=pltpu.SMEM),
            pl.BlockSpec((nz, ab, bb), lambda i: (0, 0, 0)),
        ],
        out_specs=pl.BlockSpec((rows, ab, bb), lambda i: (i, 0, 0)),
        compiler_params=pltpu.CompilerParams(vmem_limit_bytes=32 << 20),
        name="core",
    )(core_planes, gathered)
    return plane_sketch, row_t.T, col_t.T, core_sketch


def solution(mesh):
    in_specs = (
        P(("groups", "bz"), "bx", "by"),
        P("bz", None),
        P("bx", None),
        P("by", None),
        P("bz", None),
        P(None, "bx"),
        P(None, "by"),
    )
    out_specs = (
        P(("groups", "bz"), None),
        P(("groups", "bx"), ("by", "bz")),
        P(("groups", "by"), ("bx", "bz")),
        P(("groups", "bz"), "bx", "by"),
    )
    sizes = [mesh.shape[name] for name in ("bx", "by", "bz")]
    return jax.shard_map(
        functools.partial(on_device, *sizes),
        mesh=mesh, in_specs=in_specs, out_specs=out_specs, check_vma=False,
    )
```

time: 130 us -> 50.5 us (0.39)
  Pallas kernels: 0 us -> 41.1 us
  matrix products: 40.2 us -> 0 us
  local copies, waits for them, and re-layouts: 37 us -> 8.36 us
  blocking collectives: 23.1 us -> 0 us
  waiting for transfers between devices: 14.5 us -> 0 us
  between operations: 13.8 us -> 0.66 us
    pallas_call x0 -> x2, Pallas kernels: none -> 41.1 us  [the longest x1 25.2 us: on_device(): pl.pallas_call(functools.partial(exchange_kernel, nx, ny, nz), out_shape=...]
    dot_general x5 -> x0, matrix products: 40.2 us -> none  [the longest x1 30.9 us: on_device(): jnp.einsum('cp,pab->cab', core_planes, lax.all_gather(partial_value, 'bz'...]
    unnamed x6 -> x16, local copies, waits for them, and re-layouts: 36 us -> 8.36 us
    psum x1 -> x0, blocking collectives: 21.1 us -> none  [on_device(): plane_sketch = lax.psum(plane_part, ('bx', 'by'))]
    reduce_scatter x3 -> x0, waiting for transfers between devices: 14.5 us -> none  [the longest x1 14.5 us: on_device(): reduced = lax.psum_scatter(shrunk, 'by', scatter_dimension=2, tiled=True)]
    all_gather x1 -> x0, blocking collectives: 1.99 us -> none  [on_device(): lax.all_gather(partial_value, 'bz', axis=0, tiled=True)]
  transfers between devices with their start and end apart: 4 -> 0, of which waited for: 1 -> 0; matrix products, arithmetic and copies ran while one was open for 55% -> 0% of each run, Pallas kernels for 0% -> 0%
where the time goes in v1:
time: 50.5 us; the launch traced here: 50.1 us
  Pallas kernels  41.1 us (81%)
  local copies, waits for them, and re-layouts  8.36 us (17%)
  between operations  0.66 us (1%)
    pallas_call x1, Pallas kernels, on_device(): pl.pallas_call(functools.partial(exchange_kernel, nx, ny, nz), out_shape=...  25.2 us
    pallas_call x1, Pallas kernels, on_device(): pl.pallas_call(core_kernel, grid=(depth // rows,), out_shape=shape(depth,...  15.9 us
    unnamed x16, local copies, waits for them, and re-layouts  8.36 us

profile of v1, /device:TPU:0, one launch (start us, length us, event | category | flops | bytes accessed | tf_op | source)
XLA Modules:
  0.0 50.1 jit_solution(4091879723857641259)
XLA Ops:
  0.6 0.8 %copy.11.planes_ref = f32[256,2]{1,0:T(8,128)S(1)} copy(f32[256,2]{0,1:T(2,128)} %param.11) | data formatting | bytes 4096 | tf_op args[4]
  1.4 0.0 copy-start
  1.5 1.2 %copy-done = f32[512,512]{1,0:T(8,128)S(1)} copy-done((f32[512,512]{1,0:T(8,128)S(1)}, f32[512,512]{1,0:T(8,128)}, u32[]{:S(2)}) %copy-start) | copy-done | bytes 1048600
  2.7 0.0 copy-start.1
  2.7 1.0 %copy-done.1 = f32[512,256]{1,0:T(8,128)S(1)} copy-done((f32[512,256]{1,0:T(8,128)S(1)}, f32[512,256]{1,0:T(8,128)}, u32[]{:S(2)}) %copy-start.1) | copy-done | bytes 524312
  3.7 0.0 copy-start.2
  3.7 0.9 %copy-done.2 = f32[1,128,512]{2,1,0:T(8,128)S(1)} copy-done((f32[1,128,512]{2,1,0:T(8,128)S(1)}, f32[1,128,512]{2,1,0:T(8,128)}, u32[]{:S(2)}) %copy-start.2) | copy-done | bytes 262168
  4.7 0.0 copy-start.3
  4.7 0.9 %copy-done.3 = f32[512,128]{1,0:T(8,128)S(1)} copy-done((f32[512,128]{1,0:T(8,128)S(1)}, f32[512,128]{1,0:T(8,128)}, u32[]{:S(2)}) %copy-start.3) | copy-done | bytes 262168
  5.6 0.0 copy-start.4
  5.6 0.9 %copy-done.4 = f32[128,256]{1,0:T(8,128)S(1)} copy-done((f32[128,256]{1,0:T(8,128)S(1)}, f32[128,256]{1,0:T(8,128)}, u32[]{:S(2)}) %copy-start.4) | copy-done | bytes 131096
  6.5 0.0 copy-start.5
  6.5 0.7 %copy-done.5 = f32[1,256]{1,0:T(1,128)S(1)} copy-done((f32[1,256]{1,0:T(1,128)S(1)}, f32[1,256]{1,0:T(1,128)}, u32[]{:S(2)}) %copy-start.5) | copy-done | bytes 1048
  7.2 25.2 %exchange.1 = (f32[2,128,256]{2,1,0:T(8,128)S(1)}, f32[64,128]{1,0:T(8,128)S(1)}, f32[32,512]{1,0:T(8,128)S(1)}, f32[1,256]{1,0:T(1,128)S(1)}) custom-call(f32[1,128,512]{2,1,0:T(8,128)S(1)} %copy-done.2, f32[1,256]{1,0:T(1,128)S(1)} %copy-done.5, f32[128,256]{1,0:T(8,128)S(1)} %copy-done.4, f32[512,256]{1,0:T(8,128)S(1)} %copy-done.1, ...), custom_call_target="tpu_custom_call" | custom-call | tf_op jit(solution)/shard_map/exchange/pallas_call | solution.py:190
  32.4 15.9 %core.1 = f32[256,128,256]{2,1,0:T(8,128)} custom-call(f32[256,2]{1,0:T(8,128)S(1)} %copy.11.planes_ref, f32[2,128,256]{2,1,0:T(8,128)S(1)} %get-tuple-element.11.gathered_ref), custom_call_target="tpu_custom_call" | custom-call | tf_op jit(solution)/shard_map/core/pallas_call | solution.py:215
  48.3 0.6 %copy.15 = f32[1,256]{1,0:T(1,128)} copy(f32[1,256]{1,0:T(1,128)S(1)} %get-tuple-element.16) | data formatting | bytes 2048
  48.9 0.6 %copy.16 = f32[128,64]{0,1:T(8,128)} copy(f32[128,64]{0,1:T(8,128)S(1)} %bitcast.3) | data formatting | bytes 65536
  49.5 0.6 %copy.17 = f32[512,32]{0,1:T(8,128)} copy(f32[512,32]{0,1:T(8,128)S(1)} %bitcast.2) | data formatting | bytes 131072
Async XLA Ops:
  1.4 1.2 %copy-start = (f32[512,512]{1,0:T(8,128)S(1)}, f32[512,512]{1,0:T(8,128)}, u32[]{:S(2)}) copy-start(f32[512,512]{1,0:T(8,128)} %core_cols_ref.1) | copy-start | bytes 3145732
  2.7 1.0 %copy-start.1 = (f32[512,256]{1,0:T(8,128)S(1)}, f32[512,256]{1,0:T(8,128)}, u32[]{:S(2)}) copy-start(f32[512,256]{1,0:T(8,128)} %col_test_ref.1) | copy-start | bytes 1572868
  3.7 0.9 %copy-start.2 = (f32[1,128,512]{2,1,0:T(8,128)S(1)}, f32[1,128,512]{2,1,0:T(8,128)}, u32[]{:S(2)}) copy-start(f32[1,128,512]{2,1,0:T(8,128)} %slab_ref.1) | copy-start | bytes 786436
  4.7 0.9 %copy-start.3 = (f32[512,128]{1,0:T(8,128)S(1)}, f32[512,128]{1,0:T(8,128)}, u32[]{:S(2)}) copy-start(f32[512,128]{1,0:T(8,128)} %core_rows_ref.1) | copy-start | bytes 786436
  5.6 0.9 %copy-start.4 = (f32[128,256]{1,0:T(8,128)S(1)}, f32[128,256]{1,0:T(8,128)}, u32[]{:S(2)}) copy-start(f32[128,256]{1,0:T(8,128)} %row_test_ref.1) | copy-start | bytes 393220
  6.5 0.7 %copy-start.5 = (f32[1,256]{1,0:T(1,128)S(1)}, f32[1,256]{1,0:T(1,128)}, u32[]{:S(2)}) copy-start(f32[1,256]{1,0:T(1,128)} %plane_test_ref.1) | copy-start | bytes 3076

commit v2 on v1

v2 whole, which is shorter than its diff:
```python
import functools

import jax
import jax.numpy as jnp
from jax import lax
from jax.experimental import pallas as pl
from jax.experimental.pallas import tpu as pltpu
from jax.sharding import PartitionSpec as P

F32 = jnp.float32
MESH = pl.DeviceIdType.MESH


def split(x):
    high = x.astype(jnp.bfloat16)
    return high, (x - high.astype(F32)).astype(jnp.bfloat16)


def dot3(a, b, dims):
    f = functools.partial(
        lax.dot_general, dimension_numbers=(dims, ((), ())), preferred_element_type=F32
    )
    return f(a[0], b[0]) + (f(a[0], b[1]) + f(a[1], b[0]))


NN = ((1,), (0,))
NT = ((1,), (1,))


def exchange_kernel(
    nx, ny, nz,
    slab_hbm, plane_test_hbm, row_test_hbm, col_test_hbm, core_rows_hbm, core_cols_hbm,
    gathered_ref, row_ref, col_ref, plane_ref,
    slab_ref, plane_test_ref, row_test_ref, col_test_ref, core_rows_ref, core_cols_ref,
    shrunk, shrunk_in, part, part_in, full, full_in,
    row_a, row_a_in, row_b, row_b_in,
    col_a, col_a_in, col_b, col_b_in,
    plane_a, plane_a_in, plane_b, plane_b_in,
    send_sem, recv_sem, load_sem,
):
    size = {"bx": nx, "by": ny, "bz": nz}
    me = {name: lax.axis_index(name) for name in size}
    count = [0]

    loads = {}
    order = (
        (core_cols_hbm, core_cols_ref), (slab_hbm, slab_ref), (row_test_hbm, row_test_ref),
        (plane_test_hbm, plane_test_ref), (core_rows_hbm, core_rows_ref), (col_test_hbm, col_test_ref),
    )
    for n, (source, target) in enumerate(order):
        loads[n] = pltpu.make_async_copy(source, target, load_sem.at[n])
        loads[n].start()

    def peer(name, d):
        return lax.rem(me[name] + d, size[name])

    barrier = pltpu.get_barrier_semaphore()
    for name in size:
        for d in range(1, size[name]):
            pl.semaphore_signal(barrier, inc=1, device_id={name: peer(name, d)}, device_id_type=MESH)

    copies = []

    def send(name, d, src, dst):
        n = count[0]
        count[0] += 1
        copy = pltpu.make_async_remote_copy(
            src_ref=src, dst_ref=dst, send_sem=send_sem.at[n], recv_sem=recv_sem.at[n],
            device_id={name: peer(name, d)}, device_id_type=MESH,
        )
        copy.start()
        copies.append(copy)
        return copy

    def send_all(name, source, landing):
        return [send(name, d, source(d), landing(d - 1)) for d in range(1, size[name])]

    def arrived(group):
        for copy in group:
            copy.wait_recv()

    loads[0].wait()
    loads[1].wait()
    slab = split(slab_ref[0])
    chunks, ni, wide = shrunk.shape[1:]

    def shrink(h):
        rows = [
            core_cols_ref[(y * chunks + h) * wide:(y * chunks + h + 1) * wide, :] for y in range(ny)
        ]
        terms = dot3(slab, split(jnp.concatenate(rows, axis=0)), NT)
        for y in range(ny):
            shrunk[y, h] = terms[:, y * wide:(y + 1) * wide]

    def send_shrunk(h):
        return send_all("by", lambda d: shrunk.at[peer("by", d), h], lambda n: shrunk_in.at[n, h])

    shrunk_sent = []
    shrink(0)
    pl.semaphore_wait(barrier, nx + ny + nz - 3)
    shrunk_sent.append(send_shrunk(0))

    loads[2].wait()
    loads[3].wait()
    row_test = row_test_ref[...]
    plane_test = plane_test_ref[...]
    scaled = split((row_test * plane_test).T)
    terms = dot3(scaled, slab, NN)
    block = col_a.shape[2]
    for x in range(nx):
        for z in range(nz):
            first = (x * nz + z) * block
            col_a[z, x] = terms[first:first + block, :]
    col_a_sent = send_all("bz", lambda d: col_a.at[peer("bz", d)], lambda n: col_a_in.at[n])

    for h in range(1, chunks):
        shrink(h)
        shrunk_sent.append(send_shrunk(h))

    loads[4].wait()
    tall = part.shape[2]
    part_sent = []

    def send_part(h):
        arrived(shrunk_sent[h])
        total = shrunk[me["by"], h]
        for d in range(1, ny):
            total = total + shrunk_in[d - 1, h]
        reduced = split(total)
        group = []
        for d in range(1, nx + 1):
            to = peer("bx", d)
            rows = core_rows_ref[pl.ds(pl.multiple_of(to * tall, tall), tall), :]
            part[d - 1, h] = dot3(split(rows), reduced, NN)
            if d < nx:
                group.append(send("bx", d, part.at[d - 1, h], part_in.at[d - 1, h]))
        part_sent.append(group)

    send_part(0)

    arrived(col_a_sent)
    total = col_a[me["bz"]]
    for d in range(1, nz):
        total = total + col_a_in[d - 1]
    col_b[...] = total
    col_b_sent = send_all("bx", lambda d: col_b.at[peer("bx", d)], lambda n: col_b_in.at[n])

    for h in range(1, chunks):
        send_part(h)

    loads[5].wait()
    by_col = dot3(slab, split(col_test_ref[...]), NN)
    plane_a[...] = jnp.sum(by_col * row_test, axis=0, keepdims=True)
    plane_a_sent = send_all("by", lambda d: plane_a, lambda n: plane_a_in.at[n])
    terms = (by_col * plane_test).T
    block = row_a.shape[2]
    for y in range(ny):
        for z in range(nz):
            first = (y * nz + z) * block
            row_a[z, y] = terms[first:first + block, :]
    row_a_sent = send_all("bz", lambda d: row_a.at[peer("bz", d)], lambda n: row_a_in.at[n])

    arrived(plane_a_sent)
    total = plane_a[...]
    for d in range(1, ny):
        total = total + plane_a_in[d - 1]
    plane_b[...] = total
    plane_b_sent = send_all("bx", lambda d: plane_b, lambda n: plane_b_in.at[n])

    arrived(row_a_sent)
    total = row_a[me["bz"]]
    for d in range(1, nz):
        total = total + row_a_in[d - 1]
    row_b[...] = total
    row_b_sent = send_all("by", lambda d: row_b.at[peer("by", d)], lambda n: row_b_in.at[n])

    def finish_part(h):
        total = part[nx - 1, h]
        for d in range(1, nx):
            part_sent[h][d - 1].wait_recv()
            total = total + part_in[d - 1, h]
        full[h] = total
        gathered_ref[me["bz"], :, h * wide:(h + 1) * wide] = total
        return send_all("bz", lambda d: full.at[h], lambda n: full_in.at[n, h])

    full_sent = [finish_part(0)]

    arrived(row_b_sent)
    total = row_b[me["by"]]
    for d in range(1, ny):
        total = total + row_b_in[d - 1]
    row_ref[...] = total

    arrived(col_b_sent)
    total = col_b[me["bx"]]
    for d in range(1, nx):
        total = total + col_b_in[d - 1]
    col_ref[...] = total

    for h in range(1, chunks):
        full_sent.append(finish_part(h))

    arrived(plane_b_sent)
    total = plane_b[...]
    for d in range(1, nx):
        total = total + plane_b_in[d - 1]
    plane_ref[...] = total

    for h in range(chunks):
        arrived(full_sent[h])
        for d in range(1, nz):
            gathered_ref[peer("bz", nz - d), :, h * wide:(h + 1) * wide] = full_in[d - 1, h]
    for copy in copies:
        copy.wait_send()


def core_kernel(
    planes_ref, gathered_ref, row_in, col_in, plane_in,
    row_ref, col_ref, plane_ref, out_ref,
    slots, out_sem, small_sem,
):
    count, rows = slots.shape[:2]
    steps = out_ref.shape[0] // rows
    small = [
        pltpu.make_async_copy(source, target, small_sem.at[n])
        for n, (source, target) in enumerate(
            ((row_in, row_ref), (col_in, col_ref), (plane_in, plane_ref))
        )
    ]

    def copy(step, slot):
        return pltpu.make_async_copy(
            slots.at[slot], out_ref.at[pl.ds(step * rows, rows)], out_sem.at[slot]
        )

    def body(step, _):
        slot = lax.rem(step, count)

        @pl.when(step >= count)
        def _():
            copy(step - count, slot).wait()

        for c in range(rows):
            row = step * rows + c
            value = planes_ref[0, row] * gathered_ref[0]
            for p in range(1, gathered_ref.shape[0]):
                value = value + planes_ref[p, row] * gathered_ref[p]
            slots[slot, c] = value
        copy(step, slot).start()
        return 0

    lax.fori_loop(0, steps, body, 0)
    for one in small:
        one.start()
    for step in range(steps - count, steps):
        copy(step, step % count).wait()
    for one in small:
        one.wait()


def on_device(nx, ny, nz, slab, plane_test, row_test, col_test, core_planes, core_rows, core_cols):
    rank = row_test.shape[1]
    ni, nj = slab.shape[1:]
    ab, bb = core_rows.shape[0] // nx, core_cols.shape[0] // ny
    rb, cb = rank // (ny * nz), rank // (nx * nz)
    chunks = 2 if bb % 256 == 0 else 1
    wide = bb // chunks
    shape = lambda *dims: jax.ShapeDtypeStruct(dims, F32)
    vmem = lambda *dims: pltpu.VMEM(dims, F32)
    inputs = (slab, plane_test, row_test, col_test, core_rows, core_cols)
    transfers = (2 + chunks) * (nz - 1) + (2 + chunks) * (ny - 1) + (2 + chunks) * (nx - 1)
    gathered, row_t, col_t, plane_sketch = pl.pallas_call(
        functools.partial(exchange_kernel, nx, ny, nz),
        out_shape=(shape(nz, ab, bb), shape(rb, ni), shape(cb, nj), shape(1, rank)),
        in_specs=[pl.BlockSpec(memory_space=pltpu.HBM)] * 6,
        out_specs=[pl.BlockSpec(memory_space=pltpu.VMEM)] * 4,
        scratch_shapes=[vmem(*a.shape) for a in inputs] + [
            vmem(ny, chunks, ni, wide), vmem(ny - 1, chunks, ni, wide),
            vmem(nx, chunks, ab, wide), vmem(nx - 1, chunks, ab, wide),
            vmem(chunks, ab, wide), vmem(nz - 1, chunks, ab, wide),
            vmem(nz, ny, rb, ni), vmem(nz - 1, ny, rb, ni),
            vmem(ny, rb, ni), vmem(ny - 1, rb, ni),
            vmem(nz, nx, cb, nj), vmem(nz - 1, nx, cb, nj),
            vmem(nx, cb, nj), vmem(nx - 1, cb, nj),
            vmem(1, rank), vmem(ny - 1, 1, rank),
            vmem(1, rank), vmem(nx - 1, 1, rank),
            pltpu.SemaphoreType.DMA((transfers,)),
            pltpu.SemaphoreType.DMA((transfers,)),
            pltpu.SemaphoreType.DMA((len(inputs),)),
        ],
        compiler_params=pltpu.CompilerParams(
            collective_id=0, has_side_effects=True, vmem_limit_bytes=32 << 20
        ),
        name="exchange",
    )(*(pltpu.with_memory_space_constraint(a, pltpu.HBM) for a in inputs))
    depth = core_planes.shape[0]
    rows = min(depth, max(1, (1 << 17) // (ab * bb)))
    slots = min(8, depth // rows)
    row_t, col_t, plane_sketch, core_sketch = pl.pallas_call(
        core_kernel,
        out_shape=(shape(rb, ni), shape(cb, nj), shape(1, rank), shape(depth, ab, bb)),
        in_specs=[pl.BlockSpec(memory_space=pltpu.SMEM)]
        + [pl.BlockSpec(memory_space=pltpu.VMEM)] * 4,
        out_specs=[pl.BlockSpec(memory_space=pltpu.HBM)] * 4,
        scratch_shapes=[
            vmem(slots, rows, ab, bb),
            pltpu.SemaphoreType.DMA((slots,)),
            pltpu.SemaphoreType.DMA((3,)),
        ],
        compiler_params=pltpu.CompilerParams(vmem_limit_bytes=16 << 20),
        name="core",
    )(core_planes.T, gathered, row_t, col_t, plane_sketch)
    return plane_sketch, row_t.T, col_t.T, core_sketch


def solution(mesh):
    in_specs = (
        P(("groups", "bz"), "bx", "by"),
        P("bz", None),
        P("bx", None),
        P("by", None),
        P("bz", None),
        P(None, "bx"),
        P(None, "by"),
    )
    out_specs = (
        P(("groups", "bz"), None),
        P(("groups", "bx"), ("by", "bz")),
        P(("groups", "by"), ("bx", "bz")),
        P(("groups", "bz"), "bx", "by"),
    )
    sizes = [mesh.shape[name] for name in ("bx", "by", "bz")]
    return jax.shard_map(
        functools.partial(on_device, *sizes),
        mesh=mesh, in_specs=in_specs, out_specs=out_specs, check_vma=False,
    )
```

time: 50.5 us -> 40.4 us (0.80)
  local copies, waits for them, and re-layouts: 8.36 us -> 0.68 us
  Pallas kernels: 41.1 us -> 38.9 us
    unnamed x16 -> x2, local copies, waits for them, and re-layouts: 8.36 us -> 0.68 us
    pallas_call x1, Pallas kernels: 15.9 us -> 11.6 us  [on_device(): pl.pallas_call(core_kernel, out_shape=(shape(rb, ni), shape(cb, nj), shap...]
    pallas_call x1, Pallas kernels: 25.2 us -> 27.3 us  [on_device(): pl.pallas_call(functools.partial(exchange_kernel, nx, ny, nz), out_shape=...]
where the time goes in v2:
time: 40.4 us; the launch traced here: 40.3 us
  Pallas kernels  38.9 us (96%)
  local copies, waits for them, and re-layouts  0.68 us (2%)
  between operations  0.65 us (2%)
    pallas_call x1, Pallas kernels, on_device(): pl.pallas_call(functools.partial(exchange_kernel, nx, ny, nz), out_shape=...  27.3 us
    pallas_call x1, Pallas kernels, on_device(): pl.pallas_call(core_kernel, out_shape=(shape(rb, ni), shape(cb, nj), shap...  11.6 us

profile of v2, /device:TPU:0, one launch (start us, length us, event | category | flops | bytes accessed | tf_op | source)
XLA Modules:
  0.0 40.3 jit_solution(12509319334504813247)
XLA Ops:
  0.6 27.3 %exchange.1 = (f32[2,128,256]{2,1,0:T(8,128)S(1)}, f32[64,128]{1,0:T(8,128)S(1)}, f32[32,512]{1,0:T(8,128)S(1)}, f32[1,256]{1,0:T(1,128)S(1)}) custom-call(f32[1,128,512]{2,1,0:T(8,128)} %slab_hbm.1, f32[1,256]{1,0:T(1,128)} %plane_test_hbm.1, f32[128,256]{1,0:T(8,128)} %row_test_hbm.1, f32[512,256]{1,0:T(8,128)} %col_test_hbm.1, f32[512,128]{1,0:T(8,128)} %core_rows_hbm.1, ...), custom_call_target="tpu_custom_call" | custom-call | tf_op jit(solution)/shard_map/exchange/pallas_call | solution.py:272
  28.0 0.0 copy-start
  28.0 0.7 %copy-done = f32[256,2]{0,1:T(2,128)S(1)} copy-done((f32[256,2]{0,1:T(2,128)S(1)}, f32[256,2]{0,1:T(2,128)}, u32[]{:S(2)}) %copy-start) | copy-done | bytes 2072
  28.7 11.6 %core.1 = (f32[64,128]{1,0:T(8,128)}, f32[32,512]{1,0:T(8,128)}, f32[1,256]{1,0:T(1,128)}, f32[256,128,256]{2,1,0:T(8,128)}) custom-call(f32[2,256]{1,0:T(2,128)S(1)} %bitcast.3, f32[2,128,256]{2,1,0:T(8,128)S(1)} %get-tuple-element.12.gathered_ref, f32[64,128]{1,0:T(8,128)S(1)} %get-tuple-element.13.row_in, f32[32,512]{1,0:T(8,128)S(1)} %get-tuple-element.14.col_in, ...), custom_call_target="tpu_custom_call" | custom-call | tf_op jit(solution)/shard_map/core/pallas_call | solution.py:299
Async XLA Ops:
  28.0 0.7 %copy-start = (f32[256,2]{0,1:T(2,128)S(1)}, f32[256,2]{0,1:T(2,128)}, u32[]{:S(2)}) copy-start(f32[256,2]{0,1:T(2,128)} %param.11) | copy-start | bytes 6148

commit v3 on v2

--- a/solution.py
+++ b/solution.py
@@ -30,11 +30,25 @@
 def exchange_kernel(
     nx, ny, nz,
     slab_hbm, plane_test_hbm, row_test_hbm, col_test_hbm, core_rows_hbm, core_cols_hbm,
-    gathered_ref, row_ref, col_ref, plane_ref,
+    *refs,
+):
+    gathered_ref, row_ref, plane_ref = refs[:3]
+    col_refs = refs[3:3 + nx]
+    exchange_body(
+        nx, ny, nz,
+        slab_hbm, plane_test_hbm, row_test_hbm, col_test_hbm, core_rows_hbm, core_cols_hbm,
+        gathered_ref, row_ref, col_refs, plane_ref, *refs[3 + nx:],
+    )
+
+
+def exchange_body(
+    nx, ny, nz,
+    slab_hbm, plane_test_hbm, row_test_hbm, col_test_hbm, core_rows_hbm, core_cols_hbm,
+    gathered_ref, row_ref, col_refs, plane_ref,
     slab_ref, plane_test_ref, row_test_ref, col_test_ref, core_rows_ref, core_cols_ref,
     shrunk, shrunk_in, part, part_in, full, full_in,
     row_a, row_a_in, row_b, row_b_in,
-    col_a, col_a_in, col_b, col_b_in,
+    col_a, col_a_in,
     plane_a, plane_a_in, plane_b, plane_b_in,
     send_sem, recv_sem, load_sem,
 ):
@@ -138,13 +152,6 @@
 
     send_part(0)
 
-    arrived(col_a_sent)
-    total = col_a[me["bz"]]
-    for d in range(1, nz):
-        total = total + col_a_in[d - 1]
-    col_b[...] = total
-    col_b_sent = send_all("bx", lambda d: col_b.at[peer("bx", d)], lambda n: col_b_in.at[n])
-
     for h in range(1, chunks):
         send_part(h)
 
@@ -191,11 +198,12 @@
         total = total + row_b_in[d - 1]
     row_ref[...] = total
 
-    arrived(col_b_sent)
-    total = col_b[me["bx"]]
-    for d in range(1, nx):
-        total = total + col_b_in[d - 1]
-    col_ref[...] = total
+    arrived(col_a_sent)
+    for d in range(nx):
+        total = col_a[me["bz"], peer("bx", d)]
+        for n in range(nz - 1):
+            total = total + col_a_in[n, peer("bx", d)]
+        col_refs[d][...] = total
 
     for h in range(1, chunks):
         full_sent.append(finish_part(h))
@@ -215,8 +223,8 @@
 
 
 def core_kernel(
-    planes_ref, gathered_ref, row_in, col_in, plane_in,
-    row_ref, col_ref, plane_ref, out_ref,
+    planes_ref, gathered_ref, row_in, plane_in,
+    row_ref, plane_ref, out_ref,
     slots, out_sem, small_sem,
 ):
     count, rows = slots.shape[:2]
@@ -224,7 +232,7 @@
     small = [
         pltpu.make_async_copy(source, target, small_sem.at[n])
         for n, (source, target) in enumerate(
-            ((row_in, row_ref), (col_in, col_ref), (plane_in, plane_ref))
+            ((row_in, row_ref), (plane_in, plane_ref))
         )
     ]
 
@@ -268,12 +276,12 @@
     shape = lambda *dims: jax.ShapeDtypeStruct(dims, F32)
     vmem = lambda *dims: pltpu.VMEM(dims, F32)
     inputs = (slab, plane_test, row_test, col_test, core_rows, core_cols)
-    transfers = (2 + chunks) * (nz - 1) + (2 + chunks) * (ny - 1) + (2 + chunks) * (nx - 1)
-    gathered, row_t, col_t, plane_sketch = pl.pallas_call(
+    transfers = (2 + chunks) * (nz - 1) + (2 + chunks) * (ny - 1) + (1 + chunks) * (nx - 1)
+    gathered, row_t, plane_sketch, *col_terms = pl.pallas_call(
         functools.partial(exchange_kernel, nx, ny, nz),
-        out_shape=(shape(nz, ab, bb), shape(rb, ni), shape(cb, nj), shape(1, rank)),
+        out_shape=(shape(nz, ab, bb), shape(rb, ni), shape(1, rank)) + (shape(cb, nj),) * nx,
         in_specs=[pl.BlockSpec(memory_space=pltpu.HBM)] * 6,
-        out_specs=[pl.BlockSpec(memory_space=pltpu.VMEM)] * 4,
+        out_specs=[pl.BlockSpec(memory_space=pltpu.VMEM)] * (3 + nx),
         scratch_shapes=[vmem(*a.shape) for a in inputs] + [
             vmem(ny, chunks, ni, wide), vmem(ny - 1, chunks, ni, wide),
             vmem(nx, chunks, ab, wide), vmem(nx - 1, chunks, ab, wide),
@@ -281,7 +289,6 @@
             vmem(nz, ny, rb, ni), vmem(nz - 1, ny, rb, ni),
             vmem(ny, rb, ni), vmem(ny - 1, rb, ni),
             vmem(nz, nx, cb, nj), vmem(nz - 1, nx, cb, nj),
-            vmem(nx, cb, nj), vmem(nx - 1, cb, nj),
             vmem(1, rank), vmem(ny - 1, 1, rank),
             vmem(1, rank), vmem(nx - 1, 1, rank),
             pltpu.SemaphoreType.DMA((transfers,)),
@@ -296,20 +303,26 @@
     depth = core_planes.shape[0]
     rows = min(depth, max(1, (1 << 17) // (ab * bb)))
     slots = min(8, depth // rows)
-    row_t, col_t, plane_sketch, core_sketch = pl.pallas_call(
+    col_t = col_terms[0]
+    for d in range(1, nx):
+        col_t = col_t + lax.ppermute(col_terms[d], "bx", [(x, (x + d) % nx) for x in range(nx)])
+    row_t, plane_sketch, core_sketch = pl.pallas_call(
         core_kernel,
-        out_shape=(shape(rb, ni), shape(cb, nj), shape(1, rank), shape(depth, ab, bb)),
+        out_shape=(shape(rb, ni), shape(1, rank), shape(depth, ab, bb)),
         in_specs=[pl.BlockSpec(memory_space=pltpu.SMEM)]
-        + [pl.BlockSpec(memory_space=pltpu.VMEM)] * 4,
-        out_specs=[pl.BlockSpec(memory_space=pltpu.HBM)] * 4,
+        + [pl.BlockSpec(memory_space=pltpu.VMEM)] * 3,
+        out_specs=[pl.BlockSpec(memory_space=pltpu.HBM)] * 3,
         scratch_shapes=[
             vmem(slots, rows, ab, bb),
             pltpu.SemaphoreType.DMA((slots,)),
-            pltpu.SemaphoreType.DMA((3,)),
+            pltpu.SemaphoreType.DMA((2,)),
         ],
         compiler_params=pltpu.CompilerParams(vmem_limit_bytes=16 << 20),
+        cost_estimate=pl.CostEstimate(
+            flops=4 * depth * ab * bb, bytes_accessed=4 * depth * ab * bb, transcendentals=0
+        ),
         name="core",
-    )(core_planes.T, gathered, row_t, col_t, plane_sketch)
+    )(core_planes.T, gathered, row_t, plane_sketch)
     return plane_sketch, row_t.T, col_t.T, core_sketch
 
 

time: 40.4 us -> 39.4 us (0.975)
  Pallas kernels: 38.9 us -> 33.2 us
  starting transfers between devices: 0 us -> 3.98 us
  other arithmetic: 0 us -> 0.65 us
    pallas_call x1, Pallas kernels: 27.3 us -> 21.7 us  [on_device(): pl.pallas_call(functools.partial(exchange_kernel, nx, ny, nz), out_shape=...]
    ppermute x0 -> x3, starting transfers between devices: none -> 3.98 us  [on_device(): lax.ppermute(col_terms[d], 'bx', [(x, (x + d) % nx) for x in range(nx)])]
    transpose x0 -> x1, other arithmetic: none -> 0.65 us  [on_device(): return (plane_sketch, row_t.T, col_t.T, core_sketch)]
  transfers between devices with their start and end apart: 0 -> 3, of which waited for: 0 -> 0; matrix products, arithmetic and copies ran while one was open for 0% -> 0% of each run, Pallas kernels for 0% -> 29%
where the time goes in v3:
time: 39.4 us; the launch traced here: 39.2 us
  Pallas kernels  33.2 us (84%)
  starting transfers between devices  3.98 us (10%)
  local copies, waits for them, and re-layouts  0.68 us (2%)
  between operations  0.67 us (2%)
  other arithmetic  0.65 us (2%)
    pallas_call x1, Pallas kernels, on_device(): pl.pallas_call(functools.partial(exchange_kernel, nx, ny, nz), out_shape=...  21.7 us
    pallas_call x1, Pallas kernels, on_device(): pl.pallas_call(core_kernel, out_shape=(shape(rb, ni), shape(1, rank), sha...  11.6 us
    ppermute x3, starting transfers between devices, on_device(): lax.ppermute(col_terms[d], 'bx', [(x, (x + d) % nx) for x in range(nx)])  3.98 us
  transfers between devices with their start and end apart: 3, of which 0 were waited for; matrix products, arithmetic and copies ran while one was open for 0% of the time, Pallas kernels for 29%

profile of v3, /device:TPU:0, one launch (start us, length us, event | category | flops | bytes accessed | tf_op | source)
XLA Modules:
  0.0 39.2 jit_solution(9311772063824764868)
XLA Ops:
  0.6 21.7 %exchange.1 = (f32[2,128,256]{2,1,0:T(8,128)S(1)}, f32[64,128]{1,0:T(8,128)S(1)}, f32[1,256]{1,0:T(1,128)S(1)}, f32[32,512]{1,0:T(8,128)S(1)}, f32[32,512]{1,0:T...) custom-call(f32[1,128,512]{2,1,0:T(8,128)} %slab_hbm.1, f32[1,256]{1,0:T(1,128)} %plane_test_hbm.1, ...), custom_call_target="tpu_custom_call" | custom-call | tf_op jit(solution)/shard_map/exchange/pallas_call | solution.py:280
  22.3 1.3 %collective-permute-start = (f32[32,512]{1,0:T(8,128)S(1)}, f32[32,512]{1,0:T(8,128)S(1)}, u32[]{:S(2)}, u32[]{:S(2)}) collective-permute-start(f32[32,512]{1,0:T(8,128)S(1)} %get-tuple-element.20), channel_id=1, source_target_pairs={{0,4},{4,8},{8,12},{12,0},{1,5},{5,9},{9,13},{13,1},{2,6},{6,10},{... | collective-permute-start | bytes 196616 | tf_op jit(solution)/shard_map/ppermute | solution.py:308
  23.6 1.9 %collective-permute-start.1 = (f32[32,512]{1,0:T(8,128)S(1)}, f32[32,512]{1,0:T(8,128)S(1)}, u32[]{:S(2)}, u32[]{:S(2)}) collective-permute-start(f32[32,512]{1,0:T(8,128)S(1)} %get-tuple-element.21), channel_id=1, source_target_pairs={{0,8},{4,12},{8,0},{12,4},{1,9},{5,13},{9,1},{13,5},{2,10},{6,14},... | collective-permute-start | bytes 196616 | tf_op jit(solution)/shard_map/ppermute | solution.py:308
  25.5 0.8 %collective-permute-start.2 = (f32[32,512]{1,0:T(8,128)S(1)}, f32[32,512]{1,0:T(8,128)S(1)}, u32[]{:S(2)}, u32[]{:S(2)}) collective-permute-start(f32[32,512]{1,0:T(8,128)S(1)} %get-tuple-element.22), channel_id=1, source_target_pairs={{0,12},{4,0},{8,4},{12,8},{1,13},{5,1},{9,5},{13,9},{2,14},{6,2},{... | collective-permute-start | bytes 196616 | tf_op jit(solution)/shard_map/ppermute | solution.py:308
  26.3 0.0 copy-start
  26.3 0.7 %copy-done = f32[256,2]{0,1:T(2,128)S(1)} copy-done((f32[256,2]{0,1:T(2,128)S(1)}, f32[256,2]{0,1:T(2,128)}, u32[]{:S(2)}) %copy-start) | copy-done | bytes 2072
  27.0 11.6 %core.1 = (f32[64,128]{1,0:T(8,128)}, f32[1,256]{1,0:T(1,128)}, f32[256,128,256]{2,1,0:T(8,128)}) custom-call(f32[2,256]{1,0:T(2,128)S(1)} %bitcast.4, f32[2,128,256]{2,1,0:T(8,128)S(1)} %get-tuple-element.14.gathered_ref, f32[64,128]{1,0:T(8,128)S(1)} %get-tuple-element.15.row_in, f32[1,256]{1,0:T(1,128)S(1)} %get-tuple-element.16.plane_in), custom_call_target="tpu_custom_call" | custom-call | flops 33554432 | bytes 33554432 | tf_op jit(solution)/shard_map/core/pallas_call | solution.py:309
  38.5 0.0 collective-permute-done
  38.5 0.0 collective-permute-done.1
  38.6 0.0 collective-permute-done.2
  38.6 0.7 %add_bitcast_fusion = f32[512,32]{0,1:T(8,128)} fusion(f32[32,512]{1,0:T(8,128)S(1)} %collective-permute-done.2, f32[32,512]{1,0:T(8,128)S(1)} %collective-permute-done.1, f32[32,512]{1,0:T(8,128)S(1)} %get-tuple-element.19, f32[32,512]{1,0:T(8,128)S(1)} %collective-permute-done), kind=kLoop, calls=%fused_computation | loop fusion | flops 49152 | bytes 327680 | tf_op jit(solution)/shard_map/transpose | solution.py:326
Async XLA Ops:
  22.3 16.2 %collective-permute-start = (f32[32,512]{1,0:T(8,128)S(1)}, f32[32,512]{1,0:T(8,128)S(1)}, u32[]{:S(2)}, u32[]{:S(2)}) collective-permute-start(f32[32,512]{1,0:T(8,128)S(1)} %get-tuple-element.20), channel_id=1, source_target_pairs={{0,4},{4,8},{8,12},{12,0},{1,5},{5,9},{9,13},{13,1},{2,6},{6,10},{... | collective-permute-start | bytes 196616 | tf_op jit(solution)/shard_map/ppermute | solution.py:308
  23.6 14.9 %collective-permute-start.1 = (f32[32,512]{1,0:T(8,128)S(1)}, f32[32,512]{1,0:T(8,128)S(1)}, u32[]{:S(2)}, u32[]{:S(2)}) collective-permute-start(f32[32,512]{1,0:T(8,128)S(1)} %get-tuple-element.21), channel_id=1, source_target_pairs={{0,8},{4,12},{8,0},{12,4},{1,9},{5,13},{9,1},{13,5},{2,10},{6,14},... | collective-permute-start | bytes 196616 | tf_op jit(solution)/shard_map/ppermute | solution.py:308
  25.5 13.0 %collective-permute-start.2 = (f32[32,512]{1,0:T(8,128)S(1)}, f32[32,512]{1,0:T(8,128)S(1)}, u32[]{:S(2)}, u32[]{:S(2)}) collective-permute-start(f32[32,512]{1,0:T(8,128)S(1)} %get-tuple-element.22), channel_id=1, source_target_pairs={{0,12},{4,0},{8,4},{12,8},{1,13},{5,1},{9,5},{13,9},{2,14},{6,2},{... | collective-permute-start | bytes 196616 | tf_op jit(solution)/shard_map/ppermute | solution.py:308
  26.3 0.7 %copy-start = (f32[256,2]{0,1:T(2,128)S(1)}, f32[256,2]{0,1:T(2,128)}, u32[]{:S(2)}) copy-start(f32[256,2]{0,1:T(2,128)} %param.11) | copy-start | bytes 6148

commit v4 on v3

--- a/solution.py
+++ b/solution.py
@@ -33,18 +33,18 @@
     *refs,
 ):
     gathered_ref, row_ref, plane_ref = refs[:3]
-    col_refs = refs[3:3 + nx]
+    col_ref = refs[3]
     exchange_body(
         nx, ny, nz,
         slab_hbm, plane_test_hbm, row_test_hbm, col_test_hbm, core_rows_hbm, core_cols_hbm,
-        gathered_ref, row_ref, col_refs, plane_ref, *refs[3 + nx:],
+        gathered_ref, row_ref, col_ref, plane_ref, *refs[4:],
     )
 
 
 def exchange_body(
     nx, ny, nz,
     slab_hbm, plane_test_hbm, row_test_hbm, col_test_hbm, core_rows_hbm, core_cols_hbm,
-    gathered_ref, row_ref, col_refs, plane_ref,
+    gathered_ref, row_ref, col_ref, plane_ref,
     slab_ref, plane_test_ref, row_test_ref, col_test_ref, core_rows_ref, core_cols_ref,
     shrunk, shrunk_in, part, part_in, full, full_in,
     row_a, row_a_in, row_b, row_b_in,
@@ -199,11 +199,10 @@
     row_ref[...] = total
 
     arrived(col_a_sent)
-    for d in range(nx):
-        total = col_a[me["bz"], peer("bx", d)]
-        for n in range(nz - 1):
-            total = total + col_a_in[n, peer("bx", d)]
-        col_refs[d][...] = total
+    total = col_a[me["bz"]]
+    for d in range(1, nz):
+        total = total + col_a_in[d - 1]
+    col_ref[...] = total
 
     for h in range(1, chunks):
         full_sent.append(finish_part(h))
@@ -277,11 +276,11 @@
     vmem = lambda *dims: pltpu.VMEM(dims, F32)
     inputs = (slab, plane_test, row_test, col_test, core_rows, core_cols)
     transfers = (2 + chunks) * (nz - 1) + (2 + chunks) * (ny - 1) + (1 + chunks) * (nx - 1)
-    gathered, row_t, plane_sketch, *col_terms = pl.pallas_call(
+    gathered, row_t, plane_sketch, col_terms = pl.pallas_call(
         functools.partial(exchange_kernel, nx, ny, nz),
-        out_shape=(shape(nz, ab, bb), shape(rb, ni), shape(1, rank)) + (shape(cb, nj),) * nx,
+        out_shape=(shape(nz, ab, bb), shape(rb, ni), shape(1, rank)) + (shape(nx, cb, nj),),
         in_specs=[pl.BlockSpec(memory_space=pltpu.HBM)] * 6,
-        out_specs=[pl.BlockSpec(memory_space=pltpu.VMEM)] * (3 + nx),
+        out_specs=[pl.BlockSpec(memory_space=pltpu.VMEM)] * 4,
         scratch_shapes=[vmem(*a.shape) for a in inputs] + [
             vmem(ny, chunks, ni, wide), vmem(ny - 1, chunks, ni, wide),
             vmem(nx, chunks, ab, wide), vmem(nx - 1, chunks, ab, wide),
@@ -303,9 +302,7 @@
     depth = core_planes.shape[0]
     rows = min(depth, max(1, (1 << 17) // (ab * bb)))
     slots = min(8, depth // rows)
-    col_t = col_terms[0]
-    for d in range(1, nx):
-        col_t = col_t + lax.ppermute(col_terms[d], "bx", [(x, (x + d) % nx) for x in range(nx)])
+    col_t = jnp.sum(lax.all_to_all(col_terms, "bx", 0, 0, tiled=True), axis=0)
     row_t, plane_sketch, core_sketch = pl.pallas_call(
         core_kernel,
         out_shape=(shape(rb, ni), shape(1, rank), shape(depth, ab, bb)),

time: 39.4 us -> 40 us (1.015)
  Pallas kernels: 33.2 us -> 33.9 us
    ppermute x3 -> x0, starting transfers between devices: 3.98 us -> none  [on_device(): lax.ppermute(col_terms[d], 'bx', [(x, (x + d) % nx) for x in range(nx)])]
    all_to_all x0 -> x1, starting transfers between devices: none -> 3.88 us  [on_device(): col_t = jnp.sum(lax.all_to_all(col_terms, 'bx', 0, 0, tiled=True), axis=0)]
    pallas_call x1, Pallas kernels: 21.7 us -> 22.3 us  [on_device(): pl.pallas_call(functools.partial(exchange_kernel, nx, ny, nz), out_shape=...]
    transpose x1 -> x0, other arithmetic: 0.65 us -> none  [on_device(): return (plane_sketch, row_t.T, col_t.T, core_sketch)]
    reduce_sum x0 -> x1, other arithmetic: none -> 0.65 us  [on_device(): col_t = jnp.sum(lax.all_to_all(col_terms, 'bx', 0, 0, tiled=True), axis=0)]
  transfers between devices with their start and end apart: 3 -> 1, of which waited for: 0 -> 0; matrix products, arithmetic and copies ran while one was open for 0% -> 0% of each run, Pallas kernels for 29% -> 29%
where the time goes in v4:
time: 40 us; the launch traced here: 39.8 us
  Pallas kernels  33.9 us (85%)
  starting transfers between devices  3.88 us (10%)
  local copies, waits for them, and re-layouts  0.68 us (2%)
  between operations  0.66 us (2%)
  other arithmetic  0.65 us (2%)
    pallas_call x1, Pallas kernels, on_device(): pl.pallas_call(functools.partial(exchange_kernel, nx, ny, nz), out_shape=...  22.3 us
    pallas_call x1, Pallas kernels, on_device(): pl.pallas_call(core_kernel, out_shape=(shape(rb, ni), shape(1, rank), sha...  11.6 us
    all_to_all x1, starting transfers between devices, on_device(): col_t = jnp.sum(lax.all_to_all(col_terms, 'bx', 0, 0, tiled=True), axis=0)  3.88 us
  transfers between devices with their start and end apart: 1, of which 0 were waited for; matrix products, arithmetic and copies ran while one was open for 0% of the time, Pallas kernels for 29%

profile of v4, /device:TPU:0, one launch (start us, length us, event | category | flops | bytes accessed | tf_op | source)
XLA Modules:
  0.0 39.8 jit_solution(13239912602470820150)
XLA Ops:
  0.6 22.3 %exchange.1 = (f32[2,128,256]{2,1,0:T(8,128)S(1)}, f32[64,128]{1,0:T(8,128)S(1)}, f32[1,256]{1,0:T(1,128)S(1)}, f32[4,32,512]{2,1,0:T(8,128)}) custom-call(f32[1,128,512]{2,1,0:T(8,128)} %slab_hbm.1, f32[1,256]{1,0:T(1,128)} %plane_test_hbm.1, f32[128,256]{1,0:T(8,128)} %row_test_hbm.1, f32[512,256]{1,0:T(8,128)} %col_test_hbm.1, f32[512,128]{1,0:T(8,128)} %core_rows_hbm.1, ...), custom_call_target="tpu_custom_call" | custom-call | tf_op jit(solution)/shard_map/exchange/pallas_call | solution.py:279
  23.0 3.9 %all-to-all-start = ((f32[4,32,512]{2,1,0:T(8,128)}), f32[4,32,512]{2,1,0:T(8,128)S(1)}, u32[]{:S(2)}, u32[]{:S(2)}) async-start(f32[4,32,512]{2,1,0:T(8,128)} %get-tuple-element.16), calls=%async_computation | async-start | bytes 524288 | tf_op jit(solution)/shard_map/all_to_all | solution.py:305
  26.9 0.0 copy-start
  26.9 0.7 %copy-done = f32[256,2]{0,1:T(2,128)S(1)} copy-done((f32[256,2]{0,1:T(2,128)S(1)}, f32[256,2]{0,1:T(2,128)}, u32[]{:S(2)}) %copy-start) | copy-done | bytes 2072
  27.5 11.6 %core.1 = (f32[64,128]{1,0:T(8,128)}, f32[1,256]{1,0:T(1,128)}, f32[256,128,256]{2,1,0:T(8,128)}) custom-call(f32[2,256]{1,0:T(2,128)S(1)} %bitcast.3, f32[2,128,256]{2,1,0:T(8,128)S(1)} %get-tuple-element.11.gathered_ref, f32[64,128]{1,0:T(8,128)S(1)} %get-tuple-element.12.row_in, f32[1,256]{1,0:T(1,128)S(1)} %get-tuple-element.13.plane_in), custom_call_target="tpu_custom_call" | custom-call | flops 33554432 | bytes 33554432 | tf_op jit(solution)/shard_map/core/pallas_call | solution.py:306
  39.1 0.0 all-to-all-done
  39.1 0.6 %reduce_sum.9 = f32[32,512]{1,0:T(8,128)} reduce(f32[4,32,512]{2,1,0:T(8,128)S(1)} %all-to-all-done, f32[]{:T(128)} %constant.0.clone.1), dimensions={0}, to_apply=%region_0.0 | reduce | flops 49152 | bytes 327684 | tf_op jit(solution)/shard_map/reduce_sum | solution.py:305
Async XLA Ops:
  23.0 16.1 %all-to-all-start = ((f32[4,32,512]{2,1,0:T(8,128)}), f32[4,32,512]{2,1,0:T(8,128)S(1)}, u32[]{:S(2)}, u32[]{:S(2)}) async-start(f32[4,32,512]{2,1,0:T(8,128)} %get-tuple-element.16), calls=%async_computation | async-start | bytes 524288 | tf_op jit(solution)/shard_map/all_to_all | solution.py:305
  26.9 0.7 %copy-start = (f32[256,2]{0,1:T(2,128)S(1)}, f32[256,2]{0,1:T(2,128)}, u32[]{:S(2)}) copy-start(f32[256,2]{0,1:T(2,128)} %param.11) | copy-start | bytes 6148

commit v5 on v2

--- a/solution.py
+++ b/solution.py
@@ -34,7 +34,7 @@
     slab_ref, plane_test_ref, row_test_ref, col_test_ref, core_rows_ref, core_cols_ref,
     shrunk, shrunk_in, part, part_in, full, full_in,
     row_a, row_a_in, row_b, row_b_in,
-    col_a, col_a_in, col_b, col_b_in,
+    col_a, col_a_in, col_b, col_b_in, col_c, col_c_in,
     plane_a, plane_a_in, plane_b, plane_b_in,
     send_sem, recv_sem, load_sem,
 ):
@@ -61,12 +61,12 @@
 
     copies = []
 
-    def send(name, d, src, dst):
+    def send(name, d, src, dst, to=None):
         n = count[0]
         count[0] += 1
         copy = pltpu.make_async_remote_copy(
             src_ref=src, dst_ref=dst, send_sem=send_sem.at[n], recv_sem=recv_sem.at[n],
-            device_id={name: peer(name, d)}, device_id_type=MESH,
+            device_id={name: peer(name, d) if to is None else to}, device_id_type=MESH,
         )
         copy.start()
         copies.append(copy)
@@ -106,11 +106,11 @@
     plane_test = plane_test_ref[...]
     scaled = split((row_test * plane_test).T)
     terms = dot3(scaled, slab, NN)
-    block = col_a.shape[2]
+    block = col_a.shape[3]
     for x in range(nx):
         for z in range(nz):
             first = (x * nz + z) * block
-            col_a[z, x] = terms[first:first + block, :]
+            col_a[z, x % 2, x // 2] = terms[first:first + block, :]
     col_a_sent = send_all("bz", lambda d: col_a.at[peer("bz", d)], lambda n: col_a_in.at[n])
 
     for h in range(1, chunks):
@@ -143,7 +143,8 @@
     for d in range(1, nz):
         total = total + col_a_in[d - 1]
     col_b[...] = total
-    col_b_sent = send_all("bx", lambda d: col_b.at[peer("bx", d)], lambda n: col_b_in.at[n])
+    odd, pair = lax.rem(me["bx"], 2), lax.div(me["bx"], 2)
+    col_b_sent = send("bx", 1, col_b.at[1 - odd], col_b_in, to=2 * pair + 1 - odd)
 
     for h in range(1, chunks):
         send_part(h)
@@ -160,6 +161,14 @@
             row_a[z, y] = terms[first:first + block, :]
     row_a_sent = send_all("bz", lambda d: row_a.at[peer("bz", d)], lambda n: row_a_in.at[n])
 
+    half = nx // 2
+    col_b_sent.wait_recv()
+    col_c[...] = col_b[odd] + col_b_in[...]
+    col_c_sent = []
+    for d in range(1, half):
+        to = lax.rem(pair + d, half)
+        col_c_sent.append(send("bx", d, col_c.at[to], col_c_in.at[d - 1], to=2 * to + odd))
+
     arrived(plane_a_sent)
     total = plane_a[...]
     for d in range(1, ny):
@@ -191,10 +200,10 @@
         total = total + row_b_in[d - 1]
     row_ref[...] = total
 
-    arrived(col_b_sent)
-    total = col_b[me["bx"]]
-    for d in range(1, nx):
-        total = total + col_b_in[d - 1]
+    arrived(col_c_sent)
+    total = col_c[pair]
+    for d in range(1, half):
+        total = total + col_c_in[d - 1]
     col_ref[...] = total
 
     for h in range(1, chunks):
@@ -268,7 +277,7 @@
     shape = lambda *dims: jax.ShapeDtypeStruct(dims, F32)
     vmem = lambda *dims: pltpu.VMEM(dims, F32)
     inputs = (slab, plane_test, row_test, col_test, core_rows, core_cols)
-    transfers = (2 + chunks) * (nz - 1) + (2 + chunks) * (ny - 1) + (2 + chunks) * (nx - 1)
+    transfers = (2 + chunks) * (nz - 1) + (2 + chunks) * (ny - 1) + (1 + chunks) * (nx - 1) + nx // 2
     gathered, row_t, col_t, plane_sketch = pl.pallas_call(
         functools.partial(exchange_kernel, nx, ny, nz),
         out_shape=(shape(nz, ab, bb), shape(rb, ni), shape(cb, nj), shape(1, rank)),
@@ -280,8 +289,9 @@
             vmem(chunks, ab, wide), vmem(nz - 1, chunks, ab, wide),
             vmem(nz, ny, rb, ni), vmem(nz - 1, ny, rb, ni),
             vmem(ny, rb, ni), vmem(ny - 1, rb, ni),
-            vmem(nz, nx, cb, nj), vmem(nz - 1, nx, cb, nj),
-            vmem(nx, cb, nj), vmem(nx - 1, cb, nj),
+            vmem(nz, 2, nx // 2, cb, nj), vmem(nz - 1, 2, nx // 2, cb, nj),
+            vmem(2, nx // 2, cb, nj), vmem(nx // 2, cb, nj),
+            vmem(nx // 2, cb, nj), vmem(nx // 2 - 1, cb, nj),
             vmem(1, rank), vmem(ny - 1, 1, rank),
             vmem(1, rank), vmem(nx - 1, 1, rank),
             pltpu.SemaphoreType.DMA((transfers,)),

time: 40.4 us -> 38.3 us (0.948)
  Pallas kernels: 38.9 us -> 36.8 us
    pallas_call x1, Pallas kernels: 27.3 us -> 25.2 us  [on_device(): pl.pallas_call(functools.partial(exchange_kernel, nx, ny, nz), out_shape=...]
where the time goes in v5:
time: 38.3 us; the launch traced here: 38.1 us
  Pallas kernels  36.8 us (96%)
  local copies, waits for them, and re-layouts  0.68 us (2%)
  between operations  0.65 us (2%)
    pallas_call x1, Pallas kernels, on_device(): pl.pallas_call(functools.partial(exchange_kernel, nx, ny, nz), out_shape=...  25.2 us
    pallas_call x1, Pallas kernels, on_device(): pl.pallas_call(core_kernel, out_shape=(shape(rb, ni), shape(cb, nj), shap...  11.6 us

profile of v5, /device:TPU:0, one launch (start us, length us, event | category | flops | bytes accessed | tf_op | source)
XLA Modules:
  0.0 38.1 jit_solution(11097878615590472321)
XLA Ops:
  0.6 25.2 %exchange.1 = (f32[2,128,256]{2,1,0:T(8,128)S(1)}, f32[64,128]{1,0:T(8,128)S(1)}, f32[32,512]{1,0:T(8,128)S(1)}, f32[1,256]{1,0:T(1,128)S(1)}) custom-call(f32[1,128,512]{2,1,0:T(8,128)} %slab_hbm.1, f32[1,256]{1,0:T(1,128)} %plane_test_hbm.1, f32[128,256]{1,0:T(8,128)} %row_test_hbm.1, f32[512,256]{1,0:T(8,128)} %col_test_hbm.1, f32[512,128]{1,0:T(8,128)} %core_rows_hbm.1, ...), custom_call_target="tpu_custom_call" | custom-call | tf_op jit(solution)/shard_map/exchange/pallas_call | solution.py:281
  25.9 0.0 copy-start
  25.9 0.7 %copy-done = f32[256,2]{0,1:T(2,128)S(1)} copy-done((f32[256,2]{0,1:T(2,128)S(1)}, f32[256,2]{0,1:T(2,128)}, u32[]{:S(2)}) %copy-start) | copy-done | bytes 2072
  26.6 11.6 %core.1 = (f32[64,128]{1,0:T(8,128)}, f32[32,512]{1,0:T(8,128)}, f32[1,256]{1,0:T(1,128)}, f32[256,128,256]{2,1,0:T(8,128)}) custom-call(f32[2,256]{1,0:T(2,128)S(1)} %bitcast.3, f32[2,128,256]{2,1,0:T(8,128)S(1)} %get-tuple-element.12.gathered_ref, f32[64,128]{1,0:T(8,128)S(1)} %get-tuple-element.13.row_in, f32[32,512]{1,0:T(8,128)S(1)} %get-tuple-element.14.col_in, ...), custom_call_target="tpu_custom_call" | custom-call | tf_op jit(solution)/shard_map/core/pallas_call | solution.py:309
Async XLA Ops:
  25.9 0.7 %copy-start = (f32[256,2]{0,1:T(2,128)S(1)}, f32[256,2]{0,1:T(2,128)}, u32[]{:S(2)}) copy-start(f32[256,2]{0,1:T(2,128)} %param.11) | copy-start | bytes 6148
